TPU v7x, 128 devices: a whole 4x4x4 slice. The times are simulated.
128 devices in a mesh: shard: 32 (over z, x, y_hi), tensor: 4 (over y_lo, core).
Axes of the slice: x: 4, y: 4 (y_hi: 2, y_lo: 2; y = y_hi * 2 + y_lo), z: 4, core: 2. Of those that a mesh axis runs over, the one named last changes fastest.
Arguments:
- hidden_acts: bfloat16 [2, 8192, 10944], P(None, 'shard', 'tensor'), may hold values from -18 to 18
- out_grads: bfloat16 [2, 8192, 1024], P(None, 'shard'), may hold values from -18 to 18
- sample_idx: int32 [2, 4096], P(None, 'shard'), may hold values from 0 to 255
- grad_weight: bfloat16 [1024, 10944], P('shard', 'tensor'), may hold values from -112 to 112
- momentum: float32 [1024, 10944], P('shard', 'tensor'), may hold values from -6 to 6
- weight: float32 [1024, 10944], P('shard', 'tensor'), may hold values from -6 to 6
Outputs:
- new_momentum: float32 [1024, 10944], P('shard', 'tensor')
- new_weight: float32 [1024, 10944], P('shard', 'tensor')
All inputs are finite; a program needn't handle non-finite values.
Results may differ from a plain program's by a relative error of at most 0.0085.
Values may be sent and summed in bfloat16 or wider, within the bound.
A program may use at most 128 MiB of HBM per device.

v0:
```python
import jax
import jax.numpy as jnp
from jax import lax
from jax.sharding import PartitionSpec as P

DOUT = 1024
FF = 10944
ABLK = 1368
NS_STEPS = 2


DAMPING = 0.1
CLIP_LEVEL = 0.5
MOMENTUM_RATE = 0.9
LEARN_RATE = 0.5


def spread(value, axis, source):
    kept = jnp.where(lax.axis_index(axis) == source, value, 0).astype(value.dtype)
    return lax.psum(kept, axis)


def round_bf16(value):
    return lax.optimization_barrier(value.astype(jnp.bfloat16)).astype(jnp.float32)


def block_moments(rows, width, scale):
    stacked = rows.reshape(rows.shape[0], rows.shape[1] // width, width)
    moments = jnp.einsum("nkb,nkc->kbc", stacked, stacked, preferred_element_type=jnp.float32)
    return round_bf16(moments * scale)


def newton_inverse(stat):
    width = stat.shape[0]
    shift = DAMPING * jnp.trace(stat) / width
    damped = stat + shift * jnp.eye(width, dtype=jnp.float32)
    normed = (damped / jnp.sqrt(jnp.sum(damped * damped))).astype(jnp.bfloat16)
    iterate = jnp.eye(width, dtype=jnp.bfloat16)
    for step in range(NS_STEPS):
        product = jnp.dot(normed, iterate, preferred_element_type=jnp.float32).astype(jnp.bfloat16)
        twice = 2.0 * iterate.astype(jnp.float32)
        iterate = (twice - jnp.dot(iterate, product, preferred_element_type=jnp.float32)).astype(
            jnp.bfloat16
        )
    return iterate


def empty_inverse(stat):
    return jnp.zeros(stat.shape, jnp.bfloat16)


def per_device(hidden_acts, out_grads, sample_idx, grad_weight, momentum, weight):
    groups = lax.axis_size("shard")
    my_group = lax.axis_index("shard")
    batches, picks = sample_idx.shape
    scale = 1.0 / (batches * picks * groups)
    select = jax.vmap(lambda tokens, where: jnp.take(tokens, where, axis=0))
    picked_acts = select(hidden_acts, sample_idx).reshape(batches * picks, -1)
    picked_grads = select(out_grads, sample_idx).reshape(batches * picks, -1)
    act_part = block_moments(picked_acts, ABLK, scale)
    grad_part = block_moments(picked_grads, DOUT, scale)
    act_blocks = act_part.shape[0]
    stride = groups // (act_blocks + 1)
    grad_owner = act_blocks * stride
    owns_act = my_group == 0
    block = 1
    owns_act = jnp.logical_or(owns_act, my_group == block * stride)
    act_stat, grad_stat = (
        lax.psum(act_part.astype(jnp.bfloat16), "shard").astype(jnp.float32),
        lax.psum(grad_part.astype(jnp.bfloat16), "shard").astype(jnp.float32),
    )
    act_stat = round_bf16(act_stat)
    grad_block = round_bf16(grad_stat[0])
    chosen = act_stat[0]
    block = 1
    chosen = jnp.where(my_group == block * stride, act_stat[block], chosen)
    act_own = lax.cond(owns_act, newton_inverse, empty_inverse, chosen)
    grad_own = lax.cond(my_group == grad_owner, newton_inverse, empty_inverse, grad_block)
    act_inverse = jnp.stack(
        [spread(act_own, "shard", block * stride) for block in range(act_blocks)]
    )
    grad_inverse = spread(grad_own, "shard", grad_owner)
    my_rows = grad_weight.shape[0]
    first_row = my_group * my_rows
    inverse_rows = lax.dynamic_slice_in_dim(grad_inverse, first_row, my_rows, 0)
    start_total = jnp.zeros(grad_weight.shape, jnp.float32)
    piece = lax.all_gather(grad_weight, "shard", axis=0, tiled=True)
    factor_part = lax.slice_in_dim(inverse_rows, 0, piece.shape[0], axis=1)
    left = start_total + jnp.dot(factor_part, piece, preferred_element_type=jnp.float32)
    left = left.astype(jnp.bfloat16)
    hidden_width = left.shape[1]
    left_blocks = left.reshape(my_rows, act_blocks, ABLK)
    update = jnp.einsum(
        "rkb,kbc->rkc", left_blocks, act_inverse, preferred_element_type=jnp.float32
    )
    update = update.reshape(my_rows, hidden_width)
    local_align = jnp.sum(update * grad_weight.astype(jnp.float32))
    alignment = lax.psum(local_align, ("shard", "tensor"))
    ratio = jnp.minimum(1.0, CLIP_LEVEL / jnp.sqrt(alignment / (DOUT * FF)))
    new_momentum = MOMENTUM_RATE * momentum + ratio * update
    new_weight = weight - LEARN_RATE * new_momentum
    return (new_momentum, new_weight)


def solution(mesh):
    in_specs = (
        P(None, "shard", "tensor"),
        P(None, "shard", None),
        P(None, "shard"),
        P("shard", "tensor"),
        P("shard", "tensor"),
        P("shard", "tensor"),
    )
    out_specs = (P("shard", "tensor"), P("shard", "tensor"))
    return jax.shard_map(
        per_device, mesh=mesh, in_specs=in_specs, out_specs=out_specs, check_vma=False
    )
```

profile of v0, /device:TPU:1, one launch (start us, length us, event | category | flops | bytes accessed | tf_op | source)
XLA Modules:
  0.0 1105.7 jit_solution(7458162502473096947)
XLA Ops:
  7.2 0.0 copy-start
  7.2 0.0 all-reduce.7.cloned.1.call-start
  7.2 0.8 fusion.35
  8.0 0.7 fusion.51
  8.7 0.7 compare_and_fusion
  9.4 4.5 copy.13
  13.9 4.8 gather_fusion
  18.7 1.7 copy.14
  20.4 7.4 multiply_convert_fusion
  27.7 0.0 copy-done
  27.7 2.8 gather_fusion.1
  30.5 0.3 copy.15
  30.8 2.2 fusion.26
  33.0 0.0 all-reduce.7.cloned.1.call-update
  33.0 0.0 all-gather.2.cloned.1.call-start
  33.0 0.7 all-gather.2.cloned.1.call-update
  33.7 0.0 all-reduce.5.cloned.1.call-start
  33.8 444.8 %all-reduce.7.cloned.1.call-done = (bf16[2,1368,1368]{2,1,0:T(8,128)(2,1)}, bf16[1024,1024]{1,0:T(8,128)(2,1)}) async-done(((bf16[2,1368,1368]{2,1,0:T(8,128)(2,1)}, bf16[1024,1024]{1,0:T(8,128)(2,1)}), (bf16[2,1368,1368]{2,1,0:T(8,128)(2,1)}, bf16[1024,1024]{1,0:T(8,128)(2,1)})) %all-reduce.7.cloned.1.call-update) | async-done | bytes 9582864 | tf_op jit(solution)/shard_map/psum | solution.py:69
  478.6 9.7 convert_element_type.98
  488.3 0.0 copy-done.3
  488.3 2.4 convert_element_type.103
  490.7 59.7 %conditional.2 = (bf16[1368,1368]{1,0:T(8,128)(2,1)}) conditional(s32[]{:T(128)} %convert_element_type.96, () %tuple.21, (pred[]{:T(512)}, f32[2,1368,1368]{2,1,0:T(8,128)}) %tuple.22), branch_computations={%region_1.2_spmd, %region_2.5_spmd} | conditional | flops 20533264384 | bytes 59885616 | solution.py:77
  490.7 9.9 fusion
  501.3 5.8 multiply_reduce_fusion
  507.8 5.7 divide_convert_fusion
  513.5 17.4 %fusion.4 = bf16[1368,1368]{1,0:T(8,128)(2,1)} fusion(bf16[1368,1368]{1,0:T(8,128)(2,1)} %divide_convert_fusion), kind=kOutput, calls=%fused_computation.15 | convolution fusion | flops 10257275904 | bytes 7485696 | tf_op jit(solution)/shard_map/cond/branch_1_fun/dot_general | solution.py:42
  530.9 19.3 %fusion.5 = bf16[1368,1368]{1,0:T(8,128)(2,1)} fusion(bf16[1368,1368]{1,0:T(8,128)(2,1)} %fusion.4, bf16[1368,1368]{1,0:T(8,128)(2,1)} %divide_convert_fusion), kind=kOutput, calls=%fused_computation.16 | convolution fusion | flops 10249789440 | bytes 11228544 | tf_op jit(solution)/shard_map/cond/branch_1_fun/dot_general | solution.py:42
  550.5 4.0 conditional.3
  550.5 0.3 broadcast.33
  554.5 1.5 broadcast_select_fusion
  556.0 1.4 copy-done.2
  557.4 3.7 select_bitcast_fusion.1
  561.1 0.0 all-reduce.5.cloned.1.call-update
  561.2 11.1 %all-gather.2.cloned.1.call-done = bf16[1024,2736]{1,0:T(8,128)(2,1)} async-done(((bf16[32,2736]{1,0:T(8,128)(2,1)}), bf16[1024,2736]{1,0:T(8,128)(2,1)}) %all-gather.2.cloned.1.call-update) | async-done | bytes 5603344 | tf_op jit(solution)/shard_map/all_gather | solution.py:87
  572.2 447.5 %all-reduce.5.cloned.1.call-done = (bf16[1,1368,1368]{2,1,0:T(8,128)(2,1)}, bf16[1,1368,1368]{2,1,0:T(8,128)(2,1)}, bf16[1024,1024]{1,0:T(8,128)(2,1)}) async-done(((bf16[1,1368,1368]{2,1,0:T(8,128)(2,1)}, bf16[1,1368,1368]{2,1,0:T(8,128)(2,1)}, bf16[1024,1024]{1,0:T(8,128)(2,1)}), (bf16[1,1368,1368]{2,1,0:T(8,128)(2,1)}, bf16[1,1368,1368]{2,1,0:T(8,128)(2,1)}, ...) | async-done | bytes 9582864 | tf_op jit(solution)/shard_map/psum | solution.py:20
  1019.8 3.8 convolution_convert_fusion.1
  1023.5 0.2 reshape.42
  1023.8 0.0 copy-start.5
  1023.8 0.0 copy-start.6
  1023.8 0.0 copy-start.7
  1023.8 0.0 copy-start.1
  1023.8 4.7 fusion.23
  1028.5 0.3 copy.18
  1028.8 0.3 reshape.43
  1029.1 0.0 copy-done.5
  1029.1 0.7 multiply_reduce_fusion.2
  1029.8 67.3 %psum.47 = f32[]{:T(128)} all-reduce(f32[]{:T(128)} %multiply_reduce_fusion.2), channel_id=1, replica_groups=mesh['shard'=32,'tensor'=4] {'shard','tensor'}, use_global_device_ids=true, to_apply=%region_14.15 | all-reduce | flops 1 | bytes 8 | tf_op jit(solution)/shard_map/psum | solution.py:98
  1097.8 0.9 multiply_subtract_fusion
  (5 shorter events, 0.0 us)
Async XLA Ops:
  7.2 20.6 %copy-start = (bf16[2,256,1024]{2,1,0:T(8,128)(2,1)S(1)}, bf16[2,256,1024]{2,1,0:T(8,128)(2,1)}, u32[]{:S(2)}) copy-start(bf16[2,256,1024]{2,1,0:T(8,128)(2,1)} %param.11) | copy-start | bytes 3145732
  7.2 471.4 %all-reduce.7.cloned.1.call-start = ((), (), s32[]{:S(2)}) async-start(), calls=%async_computation.2 | async-start | bytes 19603456 | tf_op jit(solution)/shard_map/psum | solution.py:69
  33.0 539.2 %all-gather.2.cloned.1.call-start = ((), (), s32[]{:S(2)}) async-start(), calls=%async_computation | async-start | bytes 5947392 | tf_op jit(solution)/shard_map/all_gather | solution.py:87
  33.7 986.0 %all-reduce.5.cloned.1.call-start = ((), (), s32[]{:S(2)}) async-start(), calls=%async_computation.1 | async-start | bytes 19603456 | tf_op jit(solution)/shard_map/psum | solution.py:20
  478.6 9.7 copy-start.3
  554.5 2.8 copy-start.2
  1023.8 5.3 copy-start.5
  1023.8 74.0 %copy-start.6 = (f32[32,2736]{1,0:T(8,128)S(1)}, f32[32,2736]{1,0:T(8,128)}, u32[]{:S(2)}) copy-start(f32[32,2736]{1,0:T(8,128)} %param.15) | copy-start | bytes 1050628
  1023.8 74.0 %copy-start.7 = (f32[32,2736]{1,0:T(8,128)S(1)}, f32[32,2736]{1,0:T(8,128)}, u32[]{:S(2)}) copy-start(f32[32,2736]{1,0:T(8,128)} %param.14) | copy-start | bytes 1050628
  1023.8 74.9 %copy-start.1 = (bf16[2,256,1024]{2,1,0:T(8,128)(2,1)S(1)}, bf16[2,256,1024]{2,1,0:T(8,128)(2,1)}, u32[]{:S(2)}) copy-start(bf16[2,256,1024]{2,1,0:T(8,128)(2,1)} %param.11) | copy-start | bytes 3145732
Sparse Core Ops, SparseCore 0:
  33.1 445.4 all-reduce.6
  481.7 90.5 all-gather.1
  575.0 444.7 all-reduce.4
where the time goes:
time: 1120 us; the launch traced here: 1110 us
  waiting for transfers between devices  904 us (81%)
  blocking collectives  67.3 us (6%)
  matrix products  54.8 us (5%)
  other arithmetic  42.6 us (4%)
  local copies, waits for them, and re-layouts  16.4 us (1%)
  between operations  15.1 us (1%)
    psum x1, waiting for transfers between devices, spread(): return lax.psum(kept, axis)  448 us
    psum x1, waiting for transfers between devices, per_device(): lax.psum(act_part.astype(jnp.bfloat16), 'shard').astype(jnp.float32)  445 us
    psum x1, blocking collectives, per_device(): alignment = lax.psum(local_align, ('shard', 'tensor'))  67.3 us
    dot_general x2, matrix products, newton_inverse(): jnp.dot(iterate, product, preferred_element_type=jnp.float32)  36.8 us
  transfers between devices with their start and end apart: 3, of which 3 were waited for; matrix products, arithmetic and copies ran while one was open for 7% of the time, Pallas kernels for 0%

commit v1 on v0

v1 whole, which is shorter than its diff:
```python
import jax
import jax.numpy as jnp
from jax import lax
from jax.experimental import pallas as pl
from jax.experimental.pallas import tpu as pltpu
from jax.sharding import PartitionSpec as P

DOUT = 1024
FF = 10944
ABLK = 1368
DAMPING = 0.1
CLIP_LEVEL = 0.5
MOMENTUM_RATE = 0.9
LEARN_RATE = 0.5

F32 = jnp.float32
BF16 = jnp.bfloat16
MESH = pl.DeviceIdType.MESH

NT = 11
WIDTH = NT * 128
SPLIT = 1280
EDGE = ABLK - SPLIT
TAIL = 2 * ABLK - 2688
BAND = 6 * 128
ROWS = 96
HALF = ROWS // 2
GT = DOUT // 128
GBAND = 5 * 128
GROWS = 16
MINE = 32


def dot(a, b):
    return lax.dot_general(a, b, (((1,), (0,)), ((), ())), preferred_element_type=F32)


def dot_tn(a, b):
    return lax.dot_general(a, b, (((0,), (0,)), ((), ())), preferred_element_type=F32)


def fold_rows(value):
    return value.reshape(value.shape[0] // 8, 8, value.shape[1]).sum(0)


def total(value):
    return jnp.sum(jnp.sum(value, axis=1, keepdims=True), axis=0, keepdims=True)


def kernel(
    idx_ref, grads_ref, w_ref, acts_ref,
    upd_out, align_out,
    picked, gpicked, part, w2, wpair, wc, edge,
    gq, grecv, gall, gfull,
    rb1, st1, r1, rb2, st2, r2, r3,
    ag, sfull, vt, vfull, left, upd, ux, al, al1, al2,
    grs_s, grs_r, gag_s, gag_r, gx_s, gx_r, wa_s, wa_r, lf_s, lf_r,
    ring_s, ring_r, a1_s, a1_r, a2_s, a2_r, one_s, one_r,
):
    s = lax.axis_index("shard")
    t = lax.axis_index("tensor")
    z, x, h, o = s // 8, (s // 2) % 4, s % 2, s // 2
    pair = o * 2 + (1 - h)
    scale = 1.0 / 8192.0
    lane = lax.broadcasted_iota(jnp.int32, (1, 128), 1)

    def copy_to(src, dst, send, recv, shard, tensor=None):
        return pltpu.make_async_remote_copy(
            src_ref=src, dst_ref=dst, send_sem=send, recv_sem=recv,
            device_id=(shard, t if tensor is None else tensor), device_id_type=MESH,
        )

    def wait_bytes(ref, sem):
        pltpu.make_async_copy(ref, ref, sem).wait()

    barrier = pltpu.get_barrier_semaphore()

    @pl.loop(0, 32)
    def _(i):
        @pl.when(i != s)
        def _():
            pl.semaphore_signal(barrier, inc=1, device_id=(i, t), device_id_type=MESH)

    for d in range(1, 4):
        pl.semaphore_signal(barrier, inc=1, device_id=(s, (t + d) % 4), device_id_type=MESH)

    hots = []
    for m in range(2):
        token = lax.broadcasted_iota(jnp.int32, (256, 128), 0)
        hots.append(jnp.where(token == idx_ref[m:m + 1, :], 1.0, 0.0).astype(BF16))
    for m in range(2):
        rows = slice(128 * m, 128 * m + 128)
        pg = dot_tn(hots[m], grads_ref[m]).astype(BF16)
        gpicked[rows, 0:DOUT] = pg
        gpicked[rows, DOUT:DOUT + 512] = pg[:, 0:512]
    for i in range(2):
        at = pl.multiple_of(128 * (2 * t + i), 128)
        strip = dot_tn(gpicked[:, pl.ds(at, 128)], gpicked[:, pl.ds(at, GBAND)])
        gq[128 * i:128 * i + 128, :] = (strip * scale).astype(BF16)

    for j in range(NT - 1):
        w2[0, j] = w_ref[:, 128 * j:128 * j + 128]
        w2[1, j] = w_ref[:, WIDTH + 128 * j:WIDTH + 128 * j + 128]
    cut = w_ref[:, SPLIT:WIDTH].astype(F32)
    w2[0, NT - 1] = jnp.where(lane < EDGE, cut, 0.0).astype(BF16)
    edge[0:32, :] = jnp.where(lane >= EDGE, cut, 0.0)
    edge[0:32, 0:TAIL] = w_ref[:, 2688:2736].astype(F32)
    w2[1, NT - 1] = edge[0:32, :].astype(BF16)
    wpair[:, pl.ds(pl.multiple_of(32 * h, 32), 32), :] = w2[h]

    pl.semaphore_wait(barrier, 34)

    g_lane = t % 2
    is_gowner = h == g_lane

    @pl.loop(0, 16)
    def _(i):
        to = 2 * i + g_lane

        @pl.when(to != s)
        def _():
            copy_to(gq.at[pl.ds(pl.multiple_of(GROWS * i, GROWS), GROWS)], grecv.at[s],
                    grs_s.at[i], grs_r.at[0], to).start()

    for b in range(2):
        @pl.loop(0, NT)
        def _(j):
            to = 2 * j + b

            @pl.when(to != s)
            def _():
                copy_to(w2.at[b, j], wc.at[pl.ds(pl.multiple_of(32 * s, 32), 32)],
                        wa_s.at[b * NT + j], wa_r.at[0], to).start()

    active = o < NT

    @pl.when(active)
    def _():
        wc[pl.ds(pl.multiple_of(32 * s, 32), 32), :] = w2[h, jnp.minimum(o, NT - 1)]

    wp_copy = copy_to(w2.at[1 - h], wpair.at[:, pl.ds(pl.multiple_of(32 * h, 32), 32), :],
                      one_s.at[0], one_r.at[0], pair)
    wp_copy.start()

    @pl.when(is_gowner)
    def _():
        grecv[s] = gq[pl.ds(pl.multiple_of(GROWS * o, GROWS), GROWS), :]

    def ring_ids(axis):
        if axis == 0:
            return x, z * 8 + ((x + 1) % 4) * 2 + h, z * 8 + ((x + 3) % 4) * 2 + h
        return z, ((z + 1) % 4) * 8 + x * 2 + h, ((z + 3) % 4) * 8 + x * 2 + h

    part[0, 2, 3, 64:96] = jnp.zeros((32, BAND), BF16)
    part[0, 3, 3] = jnp.zeros((96, BAND), BF16)
    part[1, 3, 2, 64:96] = jnp.zeros((32, BAND), BF16)
    part[1, 3, 3] = jnp.zeros((96, BAND), BF16)

    pending = []

    def ring(k, src, dst, to):
        c = copy_to(src, dst, ring_s.at[k], ring_r.at[k], to)
        c.start()
        pending.append(c)
        return c

    phase1 = []
    for c in range(2):
        for m in range(2):
            rows = slice(128 * m, 128 * m + 128)
            if c == 0:
                pa = dot_tn(hots[m], acts_ref[m, :, 0:WIDTH])
                picked[c, rows, 0:SPLIT] = pa[:, 0:SPLIT].astype(BF16)
                edge[rows, :] = jnp.where(lane < EDGE, pa[:, SPLIT:WIDTH], 0.0)
                cut = jnp.where(lane >= EDGE, pa[:, SPLIT:WIDTH], 0.0)
                picked[c, rows, SPLIT:WIDTH] = edge[rows, :].astype(BF16)
                edge[rows, :] = cut
            else:
                pa = dot_tn(hots[m], acts_ref[m, :, WIDTH:2 * ABLK])
                picked[c, rows, 0:SPLIT] = pa[:, 0:SPLIT].astype(BF16)
                edge[rows, 0:TAIL] = pa[:, SPLIT:SPLIT + TAIL]
                picked[c, rows, SPLIT:WIDTH] = edge[rows, :].astype(BF16)
        picked[c, :, WIDTH:WIDTH + 640] = picked[c, :, 0:640]

        @pl.loop(0, NT)
        def _(i):
            at = pl.multiple_of(128 * i, 128)
            strip = dot_tn(picked[c, :, pl.ds(at, 128)], picked[c, :, pl.ds(at, BAND)])
            strip = (strip * scale).astype(BF16)
            for q in range(4):
                u = 4 * i + q
                oo = u // 3
                row = pl.multiple_of((u % 3) * 32, 32)
                zz, xx = oo // 4, oo % 4
                piece = strip[32 * q:32 * q + 32]
                if c == 0:
                    part[0, xx, zz, pl.ds(row, 32), :] = piece
                else:
                    part[1, zz, xx, pl.ds(row, 32), :] = piece

        pos, right, left_id = ring_ids(c)
        far, nxt, prv = (pos + 2) % 4, (pos + 1) % 4, (pos + 3) % 4
        k = 6 * c
        top, bottom = pl.ds(0, HALF), pl.ds(HALF, HALF)
        phase1.append([
            ring(k + 0, part.at[c, far, :, top], rb1.at[c, 0], right),
            ring(k + 1, part.at[c, far, :, bottom], rb1.at[c, 1], left_id),
            ring(k + 2, part.at[c, nxt, :, bottom], rb1.at[c, 2], right),
            ring(k + 3, part.at[c, prv, :, top], rb1.at[c, 3], left_id),
        ])

    @pl.when(is_gowner)
    def _():
        wait_bytes(grecv.at[pl.ds(0, 31)], grs_r.at[0])
        acc = grecv[0].astype(F32)
        for i in range(1, 32):
            acc = acc + grecv[i].astype(F32)
        gall[pl.ds(pl.multiple_of(256 * t + GROWS * o, GROWS), GROWS), :] = acc.astype(BF16)

        @pl.loop(0, 32)
        def _(i):
            @pl.when(i != s)
            def _():
                mine = gall.at[pl.ds(pl.multiple_of(256 * t + GROWS * o, GROWS), GROWS)]
                copy_to(mine, mine, gag_s.at[i], gag_r.at[0], i).start()

    def add2(a, b):
        return a.astype(F32) + b.astype(F32)

    def add3(a, b, c):
        return a.astype(F32) + b.astype(F32) + c.astype(F32)

    for c in range(2):
        pos, right, left_id = ring_ids(c)
        nxt, prv = (pos + 1) % 4, (pos + 3) % 4
        k = 6 * c
        phase1[c][0].wait_recv()
        for y in range(4):
            st1[c, 0, y] = add2(rb1[c, 0, y], part[c, nxt, y, 0:HALF]).astype(BF16)
        phase1[c].append(ring(k + 4, st1.at[c, 0], rb1.at[c, 4], right))
        phase1[c][1].wait_recv()
        for y in range(4):
            st1[c, 1, y] = add2(rb1[c, 1, y], part[c, prv, y, HALF:ROWS]).astype(BF16)
        phase1[c].append(ring(k + 5, st1.at[c, 1], rb1.at[c, 5], left_id))

    @pl.when(is_gowner)
    def _():
        wait_bytes(gall.at[pl.ds(0, 240)], gag_r.at[0])

    @pl.when(jnp.logical_not(is_gowner))
    def _():
        wait_bytes(gall.at[pl.ds(0, 256)], gag_r.at[0])

    gx = []
    for d in range(1, 4):
        mine = gall.at[pl.ds(pl.multiple_of(256 * t, 256), 256)]
        g = copy_to(mine, mine, gx_s.at[d], gx_r.at[d], s, (t + d) % 4)
        g.start()
        gx.append(g)

    phase2 = []
    for c in range(2):
        pos, right, left_id = ring_ids(c)
        for cp in phase1[c][2:]:
            cp.wait_recv()
        for y in range(4):
            r1[c, y, 0:HALF] = add3(part[c, pos, y, 0:HALF], rb1[c, 4, y], rb1[c, 3, y]).astype(BF16)
            r1[c, y, HALF:ROWS] = add3(part[c, pos, y, HALF:ROWS], rb1[c, 5, y], rb1[c, 2, y]).astype(BF16)
        pos, right, left_id = ring_ids(1 - c)
        far, nxt, prv = (pos + 2) % 4, (pos + 1) % 4, (pos + 3) % 4
        k = 12 + 6 * c
        phase2.append([
            ring(k + 0, r1.at[c, far, top], rb2.at[c, 0], right),
            ring(k + 1, r1.at[c, far, bottom], rb2.at[c, 1], left_id),
            ring(k + 2, r1.at[c, nxt, bottom], rb2.at[c, 2], right),
            ring(k + 3, r1.at[c, prv, top], rb2.at[c, 3], left_id),
        ])
    for c in range(2):
        pos, right, left_id = ring_ids(1 - c)
        nxt, prv = (pos + 1) % 4, (pos + 3) % 4
        k = 12 + 6 * c
        phase2[c][0].wait_recv()
        st2[c, 0] = add2(rb2[c, 0], r1[c, nxt, 0:HALF]).astype(BF16)
        phase2[c].append(ring(k + 4, st2.at[c, 0], rb2.at[c, 4], right))
        phase2[c][1].wait_recv()
        st2[c, 1] = add2(rb2[c, 1], r1[c, prv, HALF:ROWS]).astype(BF16)
        phase2[c].append(ring(k + 5, st2.at[c, 1], rb2.at[c, 5], left_id))
    for c in range(2):
        pos, right, left_id = ring_ids(1 - c)
        for cp in phase2[c][2:]:
            cp.wait_recv()
        r2[c, 0:HALF] = add3(r1[c, pos, 0:HALF], rb2[c, 4], rb2[c, 3]).astype(BF16)
        r2[c, HALF:ROWS] = add3(r1[c, pos, HALF:ROWS], rb2[c, 5], rb2[c, 2]).astype(BF16)

    hx = ring(24, r2.at[1 - h], r3, pair)
    hx.wait_recv()
    ag[pl.ds(pl.multiple_of(ROWS * o, ROWS), ROWS), :] = add2(r2[h], r3[...]).astype(BF16)

    def piece(axis, first, second, k):
        zz, xx = (second, first) if axis == 0 else (first, second)
        return ag.at[pl.ds(pl.multiple_of(ROWS * (4 * zz + xx) + HALF * k, HALF), HALF)]

    def cols(ref, side):
        return ref.at[:, pl.ds(384 * side, 384)]

    lines = []
    for k in range(2):
        pa, ra, la = ring_ids(k)
        pb, rb, lb = ring_ids(1 - k)
        base = 25 + 16 * k
        own = piece(k, pa, pb, k)
        lines.append({"a": [ring(base, own, own, ra), ring(base + 1, own, own, la)], "r": [], "l": []})

    def send_b(k, n, first):
        pb, rb, lb = ring_ids(1 - k)
        base = 25 + 16 * k
        p = piece(k, first, pb, k)
        lines[k]["r"].append(ring(base + 4 + n, p, p, rb))
        lines[k]["l"].append(ring(base + 8 + n, p, p, lb))

    for k in range(2):
        send_b(k, 0, ring_ids(k)[0])
    for k in range(2):
        pa, ra, la = ring_ids(k)
        pb = ring_ids(1 - k)[0]
        base = 25 + 16 * k
        lines[k]["a"][0].wait_recv()
        p = cols(piece(k, (pa + 3) % 4, pb, k), 0)
        lines[k]["a"].append(ring(base + 2, p, p, ra))
        lines[k]["a"][1].wait_recv()
        p = cols(piece(k, (pa + 1) % 4, pb, k), 1)
        lines[k]["a"].append(ring(base + 3, p, p, la))
    for k in range(2):
        pa = ring_ids(k)[0]
        send_b(k, 1, (pa + 3) % 4)
        send_b(k, 2, (pa + 1) % 4)
    for k in range(2):
        pa = ring_ids(k)[0]
        lines[k]["a"][2].wait_recv()
        lines[k]["a"][3].wait_recv()
        send_b(k, 3, (pa + 2) % 4)
    order = (0, 3, 1, 2)
    for n in range(2):
        for k in range(2):
            pa = ring_ids(k)[0]
            pb, rb, lb = ring_ids(1 - k)
            base = 25 + 16 * k
            lines[k]["r"][n].wait_recv()
            p = piece(k, (pa + order[n]) % 4, (pb + 3) % 4, k)
            lines[k]["a"].append(ring(base + 12 + n, p, p, rb))

    for g in gx:
        g.wait_recv()
    eye = lax.broadcasted_iota(jnp.int32, (128, 128), 0) == lax.broadcasted_iota(jnp.int32, (128, 128), 1)

    def unpack(src, dst, tiles, band, double):
        bands = band // 128
        column = lax.broadcasted_iota(jnp.int32, (1, band), 1) // 128
        weight = jnp.where(jnp.logical_and(column > 0, column <= double), 2.0, 1.0)

        def body(i, carry):
            square, trace = carry
            at = pl.multiple_of(128 * i, 128)
            strip = src[pl.ds(at, 128), :]
            wide = strip.astype(F32)
            square = square + fold_rows(wide * wide) * weight
            trace = trace + fold_rows(jnp.where(eye, wide[:, 0:128], 0.0))
            for k in range(bands):
                to = pl.multiple_of(128 * ((i + k) % tiles), 128)
                dst[pl.ds(at, 128), pl.ds(to, 128)] = strip[:, 128 * k:128 * k + 128]
                if 1 <= k <= double:
                    dst[pl.ds(to, 128), pl.ds(at, 128)] = wide[:, 128 * k:128 * k + 128].T.astype(BF16)
            return square, trace

        square, trace = lax.fori_loop(
            0, tiles, body, (jnp.zeros((8, band), F32), jnp.zeros((8, 128), F32)))
        return total(square), total(trace)

    def norms(square, trace, width):
        shift = DAMPING * trace / width
        return shift, 1.0 / jnp.sqrt(square + 2.0 * shift * trace + shift * shift * width)

    @pl.when(active)
    def _():
        square, trace = unpack(gall, gfull, GT, GBAND, 3)
        shift, inv = norms(square, trace, float(DOUT))
        wait_bytes(wc.at[pl.ds(0, 31 * 32)], wa_r.at[0])
        y0 = wc[...].astype(F32)
        y1 = (dot(gfull[...], wc[...]) + shift * y0) * inv
        left[...] = y1.astype(BF16)
        y2 = (dot(gfull[...], left[...]) + shift * y1) * inv
        left[...] = y2.astype(BF16)
        y3 = (dot(gfull[...], left[...]) + shift * y2) * inv
        left[...] = (4.0 * y0 - 6.0 * y1 + 4.0 * y2 - y3).astype(BF16)
        vt[o] = left[pl.ds(pl.multiple_of(64 * o, 64), 64), :]

        @pl.loop(0, 16)
        def _(i):
            @pl.when(i != o)
            def _():
                copy_to(left.at[pl.ds(pl.multiple_of(64 * i, 64), 64)], vt.at[o],
                        lf_s.at[i], lf_r.at[0], 2 * i + h).start()

    for n in range(2, 4):
        for k in range(2):
            pa = ring_ids(k)[0]
            pb, rb, lb = ring_ids(1 - k)
            base = 25 + 16 * k
            lines[k]["l"][n].wait_recv()
            p = piece(k, (pa + order[n]) % 4, (pb + 1) % 4, k)
            lines[k]["a"].append(ring(base + 12 + n, p, p, lb))
    for k in range(2):
        for n in range(2, 4):
            lines[k]["r"][n].wait_recv()
        for n in range(2):
            lines[k]["l"][n].wait_recv()
        for cp in lines[k]["a"][4:]:
            cp.wait_recv()

    square, trace = unpack(ag, sfull, NT, BAND, 5)
    shift, inv = norms(square, trace, float(ABLK))

    @pl.when(active)
    def _():
        wait_bytes(vt.at[pl.ds(0, NT - 1)], lf_r.at[0])

    @pl.when(jnp.logical_not(active))
    def _():
        wait_bytes(vt, lf_r.at[0])

    for j in range(NT):
        vfull[:, 128 * j:128 * j + 128] = vt[j]
    y0 = vfull[...].astype(F32)
    y1 = (dot(vfull[...], sfull[...]) + shift * y0) * inv
    vfull[...] = y1.astype(BF16)
    upd[...] = 4.0 * y0 - 6.0 * y1
    y2 = (dot(vfull[...], sfull[...]) + shift * y1) * inv
    vfull[...] = y2.astype(BF16)
    upd[...] = upd[...] + 4.0 * y2
    y3 = (dot(vfull[...], sfull[...]) + shift * y2) * inv
    upd[...] = upd[...] - y3

    u_copy = copy_to(upd.at[pl.ds(pl.multiple_of(32 * (1 - h), 32), 32)], ux, one_s.at[1], one_r.at[1], pair)
    u_copy.start()

    wp_copy.wait_recv()
    acc = jnp.zeros((64, 128), F32)
    for j in range(NT):
        acc = acc + upd[:, 128 * j:128 * j + 128] * wpair[j].astype(F32)
    al[0] = fold_rows(acc)
    al1[t] = al[0]
    sums = []
    for d in range(1, 4):
        g = copy_to(al.at[0], al1.at[t], a1_s.at[d], a1_r.at[d], s, (t + d) % 4)
        g.start()
        sums.append(g)
    for g in sums:
        g.wait_recv()
    al[1] = (al1[0] + al1[1]) + (al1[2] + al1[3])
    al2[s] = al[1]

    @pl.loop(0, 32)
    def _(i):
        @pl.when(i != s)
        def _():
            copy_to(al.at[1], al2.at[s], a2_s.at[i], a2_r.at[0], i).start()

    u_copy.wait_recv()
    own = upd[pl.ds(pl.multiple_of(32 * h, 32), 32), :]
    other = ux[...]
    b0 = jnp.where(h == 0, own, other)
    b1 = jnp.where(h == 0, other, own)
    upd_out[:, 0:SPLIT] = b0[:, 0:SPLIT]
    upd_out[:, SPLIT:WIDTH] = jnp.where(lane < EDGE, b0[:, SPLIT:WIDTH], b1[:, SPLIT:WIDTH])
    upd_out[:, WIDTH:2688] = b1[:, 0:SPLIT]
    upd_out[:, 2688:2736] = b1[:, SPLIT:SPLIT + TAIL]

    wait_bytes(al2.at[pl.ds(0, 31)], a2_r.at[0])
    acc = al2[0]
    for i in range(1, 32):
        acc = acc + al2[i]
    align_out[...] = jnp.broadcast_to(total(acc), (8, 128))

    for cp in pending + gx + sums + [wp_copy, u_copy]:
        cp.wait_send()

    @pl.loop(0, 16)
    def _(i):
        @pl.when(2 * i + g_lane != s)
        def _():
            wait_bytes(gq.at[pl.ds(0, GROWS)], grs_s.at[i])

        @pl.when(jnp.logical_and(active, i != o))
        def _():
            wait_bytes(left.at[pl.ds(0, 64)], lf_s.at[i])

    for b in range(2):
        @pl.loop(0, NT)
        def _(j):
            @pl.when(2 * j + b != s)
            def _():
                wait_bytes(w2.at[b, j], wa_s.at[b * NT + j])

    @pl.loop(0, 32)
    def _(i):
        @pl.when(i != s)
        def _():
            wait_bytes(al.at[1], a2_s.at[i])

        @pl.when(jnp.logical_and(is_gowner, i != s))
        def _():
            wait_bytes(gall.at[pl.ds(0, GROWS)], gag_s.at[i])


def whole_step(sample_idx, out_grads, grad_weight, hidden_acts):
    dma = pltpu.SemaphoreType.DMA
    vmem = pltpu.VMEM
    return pl.pallas_call(
        kernel,
        out_shape=(
            jax.ShapeDtypeStruct((MINE, 2 * ABLK), F32),
            jax.ShapeDtypeStruct((8, 128), F32),
        ),
        in_specs=[pl.BlockSpec(memory_space=pltpu.VMEM)] * 4,
        out_specs=(pl.BlockSpec(memory_space=pltpu.VMEM),) * 2,
        scratch_shapes=[
            vmem((2, 256, WIDTH + 640), BF16),
            vmem((256, DOUT + 512), BF16),
            vmem((2, 4, 4, ROWS, BAND), BF16),
            vmem((2, NT, 32, 128), BF16),
            vmem((NT, 64, 128), BF16),
            vmem((DOUT, 128), BF16),
            vmem((256, 128), F32),
            vmem((256, GBAND), BF16),
            vmem((32, GROWS, GBAND), BF16),
            vmem((DOUT, GBAND), BF16),
            vmem((DOUT, DOUT), BF16),
            vmem((2, 6, 4, HALF, BAND), BF16),
            vmem((2, 2, 4, HALF, BAND), BF16),
            vmem((2, 4, ROWS, BAND), BF16),
            vmem((2, 6, HALF, BAND), BF16),
            vmem((2, 2, HALF, BAND), BF16),
            vmem((2, ROWS, BAND), BF16),
            vmem((ROWS, BAND), BF16),
            vmem((16 * ROWS, BAND), BF16),
            vmem((WIDTH, WIDTH), BF16),
            vmem((NT, 64, 128), BF16),
            vmem((64, WIDTH), BF16),
            vmem((DOUT, 128), BF16),
            vmem((64, WIDTH), F32),
            vmem((32, WIDTH), F32),
            vmem((2, 8, 128), F32),
            vmem((4, 8, 128), F32),
            vmem((32, 8, 128), F32),
            dma((16,)), dma((1,)),
            dma((32,)), dma((1,)),
            dma((4,)), dma((4,)),
            dma((2 * NT,)), dma((1,)),
            dma((16,)), dma((1,)),
            dma((57,)), dma((57,)),
            dma((4,)), dma((4,)),
            dma((32,)), dma((1,)),
            dma((2,)), dma((2,)),
        ],
        compiler_params=pltpu.CompilerParams(
            collective_id=0, has_side_effects=True, vmem_limit_bytes=60 * 1024 * 1024),
    )(sample_idx, out_grads, grad_weight, hidden_acts)


def per_device(hidden_acts, out_grads, sample_idx, grad_weight, momentum, weight):
    update, alignment = whole_step(sample_idx, out_grads, grad_weight, hidden_acts)
    ratio = jnp.minimum(1.0, CLIP_LEVEL / jnp.sqrt(alignment[0, 0] / (DOUT * FF)))
    new_momentum = MOMENTUM_RATE * momentum + ratio * update
    new_weight = weight - LEARN_RATE * new_momentum
    return (new_momentum, new_weight)


def solution(mesh):
    in_specs = (
        P(None, "shard", "tensor"),
        P(None, "shard", None),
        P(None, "shard"),
        P("shard", "tensor"),
        P("shard", "tensor"),
        P("shard", "tensor"),
    )
    out_specs = (P("shard", "tensor"), P("shard", "tensor"))
    return jax.shard_map(
        per_device, mesh=mesh, in_specs=in_specs, out_specs=out_specs, check_vma=False
    )
```

time: 1120 us -> 106 us (0.09); the launches traced: 1110 us -> 106 us
  waiting for transfers between devices: 904 us -> 0 us
  Pallas kernels: 0 us -> 97.1 us
  blocking collectives: 67.3 us -> 0 us
  matrix products: 54.8 us -> 0 us
  other arithmetic: 42.6 us -> 1.91 us
  between operations: 15.1 us -> 1.35 us
    psum x2 -> x0, waiting for transfers between devices: 892 us -> none  [the longest x1 448 us: spread(): return lax.psum(kept, axis)]
    pallas_call x0 -> x1, Pallas kernels: none -> 97.1 us  [whole_step(): pl.pallas_call(kernel, out_shape=(jax.ShapeDtypeStruct((MINE, 2 * ABLK),...]
    psum x1 -> x0, blocking collectives: 67.3 us -> none  [per_device(): alignment = lax.psum(local_align, ('shard', 'tensor'))]
    dot_general x6 -> x0, matrix products: 54.8 us -> none  [the longest x2 36.8 us: newton_inverse(): jnp.dot(iterate, product, preferred_element_type=jnp.float32)]
    convert_element_type x3 -> x0, other arithmetic: 17.8 us -> none  [the longest x2 12.1 us: round_bf16(): lax.optimization_barrier(value.astype(jnp.bfloat16)).astype(jnp.float32)]
    reduce_sum x3 -> x0, other arithmetic: 16.5 us -> none  [the longest x1 9.93 us: newton_inverse(): shift = DAMPING * jnp.trace(stat) / width]
  transfers between devices with their start and end apart: 3 -> 0, of which waited for: 3 -> 0; matrix products, arithmetic and copies ran while one was open for 7% -> 0% of each run, Pallas kernels for 0% -> 0%
where the time goes in v1:
time: 106 us
  Pallas kernels  97.1 us (92%)
  local copies, waits for them, and re-layouts  5.73 us (5%)
  other arithmetic  1.91 us (2%)
  between operations  1.35 us (1%)
    pallas_call x1, Pallas kernels, whole_step(): pl.pallas_call(kernel, out_shape=(jax.ShapeDtypeStruct((MINE, 2 * ABLK),...  97.1 us
    unnamed x5, local copies, waits for them, and re-layouts  4.54 us

profile of v1, /device:TPU:1, one launch (start us, length us, event | category | flops | bytes accessed | tf_op | source)
XLA Modules:
  0.0 106.1 jit_solution(15378616322334471339)
XLA Ops:
  0.6 4.5 %copy.8.acts_ref = bf16[2,256,2736]{2,1,0:T(8,128)(2,1)} copy(bf16[2,256,2736]{1,2,0:T(8,128)(2,1)} %param.6) | data formatting | bytes 5603328 | tf_op args[0]
  5.2 0.0 copy-start
  5.2 0.0 copy-start.1
  5.2 97.1 %shard_map.77 = (f32[32,2736]{1,0:T(8,128)}, f32[8,128]{1,0:T(8,128)}) custom-call(s32[2,128]{1,0:T(2,128)} %idx_ref.1, bf16[2,256,1024]{2,1,0:T(8,128)(2,1)} %grads_ref.1, bf16[32,2736]{1,0:T(8,128)(2,1)} %w_ref.1, bf16[2,256,2736]{2,1,0:T(8,128)(2,1)} %copy.8.acts_ref), custom_call_target="tpu_custom_call" | custom-call | tf_op jit(solution)/shard_map/pallas_call | solution.py:518
  102.3 1.2 %slice.3 = f32[1,1]{1,0:T(1,128)} slice(f32[8,128]{1,0:T(8,128)} %get-tuple-element.4), slice={[0:1], [0:1]} | slice | bytes 8 | tf_op jit(solution)/shard_map/slice | solution.py:572
  104.2 0.0 copy-done
  104.2 0.0 copy-done.1
  104.2 1.9 %multiply_subtract_fusion = (f32[32,2736]{1,0:T(8,128)}, f32[32,2736]{1,0:T(8,128)}) fusion(f32[32,2736]{1,0:T(8,128)S(1)} %copy-done, f32[32,2736]{1,0:T(8,128)} %get-tuple-element.5, f32[]{:T(128)} %bitcast, f32[32,2736]{1,0:T(8,128)S(1)} %copy-done.1), kind=kLoop, calls=%fused_computation | loop fusion | flops 437760 | bytes 1751044 | tf_op jit(solution)/shard_map/sub | solution.py:574
Async XLA Ops:
  5.2 99.0 %copy-start = (f32[32,2736]{1,0:T(8,128)S(1)}, f32[32,2736]{1,0:T(8,128)}, u32[]{:S(2)}) copy-start(f32[32,2736]{1,0:T(8,128)} %param.11) | copy-start | bytes 1050628
  5.2 99.0 %copy-start.1 = (f32[32,2736]{1,0:T(8,128)S(1)}, f32[32,2736]{1,0:T(8,128)}, u32[]{:S(2)}) copy-start(f32[32,2736]{1,0:T(8,128)} %param.10) | copy-start | bytes 1050628

commit v2 on v1

--- a/solution.py
+++ b/solution.py
@@ -43,19 +43,24 @@
     return value.reshape(value.shape[0] // 8, 8, value.shape[1]).sum(0)
 
 
+def dot_nt(a, b):
+    return lax.dot_general(a, b, (((1,), (1,)), ((), ())), preferred_element_type=F32)
+
+
 def total(value):
     return jnp.sum(jnp.sum(value, axis=1, keepdims=True), axis=0, keepdims=True)
 
 
 def kernel(
-    idx_ref, grads_ref, w_ref, acts_ref,
-    upd_out, align_out,
+    idx_ref, grads_hbm, w_hbm, acts_hbm,
+    upd_out,
+    grads_ref, w_ref, acts_ref,
     picked, gpicked, part, w2, wpair, wc, edge,
     gq, grecv, gall, gfull,
     rb1, st1, r1, rb2, st2, r2, r3,
     ag, sfull, vt, vfull, left, upd, ux, al, al1, al2,
     grs_s, grs_r, gag_s, gag_r, gx_s, gx_r, wa_s, wa_r, lf_s, lf_r,
-    ring_s, ring_r, a1_s, a1_r, a2_s, a2_r, one_s, one_r,
+    ring_s, ring_r, a1_s, a1_r, a2_s, a2_r, one_s, one_r, in_s,
 ):
     s = lax.axis_index("shard")
     t = lax.axis_index("tensor")
@@ -73,6 +78,14 @@
     def wait_bytes(ref, sem):
         pltpu.make_async_copy(ref, ref, sem).wait()
 
+    loads = [
+        pltpu.make_async_copy(grads_hbm, grads_ref, in_s.at[0]),
+        pltpu.make_async_copy(w_hbm, w_ref, in_s.at[1]),
+        pltpu.make_async_copy(acts_hbm, acts_ref, in_s.at[2]),
+    ]
+    for load in loads:
+        load.start()
+
     barrier = pltpu.get_barrier_semaphore()
 
     @pl.loop(0, 32)
@@ -83,11 +96,14 @@
 
     for d in range(1, 4):
         pl.semaphore_signal(barrier, inc=1, device_id=(s, (t + d) % 4), device_id_type=MESH)
+    across = 2 * (1 - t // 2) + t % 2
+    pl.semaphore_signal(barrier, inc=1, device_id=(pair, across), device_id_type=MESH)
 
     hots = []
     for m in range(2):
         token = lax.broadcasted_iota(jnp.int32, (256, 128), 0)
         hots.append(jnp.where(token == idx_ref[m:m + 1, :], 1.0, 0.0).astype(BF16))
+    loads[0].wait()
     for m in range(2):
         rows = slice(128 * m, 128 * m + 128)
         pg = dot_tn(hots[m], grads_ref[m]).astype(BF16)
@@ -98,17 +114,18 @@
         strip = dot_tn(gpicked[:, pl.ds(at, 128)], gpicked[:, pl.ds(at, GBAND)])
         gq[128 * i:128 * i + 128, :] = (strip * scale).astype(BF16)
 
+    loads[1].wait()
     for j in range(NT - 1):
         w2[0, j] = w_ref[:, 128 * j:128 * j + 128]
         w2[1, j] = w_ref[:, WIDTH + 128 * j:WIDTH + 128 * j + 128]
     cut = w_ref[:, SPLIT:WIDTH].astype(F32)
     w2[0, NT - 1] = jnp.where(lane < EDGE, cut, 0.0).astype(BF16)
-    edge[0:32, :] = jnp.where(lane >= EDGE, cut, 0.0)
+    edge[0:32, 0:128] = jnp.where(lane >= EDGE, cut, 0.0)
     edge[0:32, 0:TAIL] = w_ref[:, 2688:2736].astype(F32)
-    w2[1, NT - 1] = edge[0:32, :].astype(BF16)
+    w2[1, NT - 1] = edge[0:32, 0:128].astype(BF16)
     wpair[:, pl.ds(pl.multiple_of(32 * h, 32), 32), :] = w2[h]
 
-    pl.semaphore_wait(barrier, 34)
+    pl.semaphore_wait(barrier, 35)
 
     g_lane = t % 2
     is_gowner = h == g_lane
@@ -157,6 +174,8 @@
     part[1, 3, 3] = jnp.zeros((96, BAND), BF16)
 
     pending = []
+    loads[2].wait()
+    high = lax.broadcasted_iota(jnp.int32, (128, 1), 0) >= EDGE
 
     def ring(k, src, dst, to):
         c = copy_to(src, dst, ring_s.at[k], ring_r.at[k], to)
@@ -167,25 +186,24 @@
     phase1 = []
     for c in range(2):
         for m in range(2):
-            rows = slice(128 * m, 128 * m + 128)
+            cols_m = slice(128 * m, 128 * m + 128)
             if c == 0:
-                pa = dot_tn(hots[m], acts_ref[m, :, 0:WIDTH])
-                picked[c, rows, 0:SPLIT] = pa[:, 0:SPLIT].astype(BF16)
-                edge[rows, :] = jnp.where(lane < EDGE, pa[:, SPLIT:WIDTH], 0.0)
-                cut = jnp.where(lane >= EDGE, pa[:, SPLIT:WIDTH], 0.0)
-                picked[c, rows, SPLIT:WIDTH] = edge[rows, :].astype(BF16)
-                edge[rows, :] = cut
+                pa = dot(acts_ref[m, 0:WIDTH, :], hots[m])
+                picked[c, 0:SPLIT, cols_m] = pa[0:SPLIT].astype(BF16)
+                cut = pa[SPLIT:WIDTH]
+                picked[c, SPLIT:WIDTH, cols_m] = jnp.where(high, 0.0, cut).astype(BF16)
+                edge[:, cols_m] = jnp.where(high, cut, 0.0)
             else:
-                pa = dot_tn(hots[m], acts_ref[m, :, WIDTH:2 * ABLK])
-                picked[c, rows, 0:SPLIT] = pa[:, 0:SPLIT].astype(BF16)
-                edge[rows, 0:TAIL] = pa[:, SPLIT:SPLIT + TAIL]
-                picked[c, rows, SPLIT:WIDTH] = edge[rows, :].astype(BF16)
-        picked[c, :, WIDTH:WIDTH + 640] = picked[c, :, 0:640]
+                pa = dot(acts_ref[m, WIDTH:2 * ABLK, :], hots[m])
+                picked[c, 0:SPLIT, cols_m] = pa[0:SPLIT].astype(BF16)
+                edge[0:TAIL, cols_m] = pa[SPLIT:SPLIT + TAIL]
+                picked[c, SPLIT:WIDTH, cols_m] = edge[:, cols_m].astype(BF16)
+        picked[c, WIDTH:WIDTH + 640, :] = picked[c, 0:640, :]
 
         @pl.loop(0, NT)
         def _(i):
             at = pl.multiple_of(128 * i, 128)
-            strip = dot_tn(picked[c, :, pl.ds(at, 128)], picked[c, :, pl.ds(at, BAND)])
+            strip = dot_nt(picked[c, pl.ds(at, 128), :], picked[c, pl.ds(at, BAND), :])
             strip = (strip * scale).astype(BF16)
             for q in range(4):
                 u = 4 * i + q
@@ -198,6 +216,22 @@
                 else:
                     part[1, zz, xx, pl.ds(row, 32), :] = piece
 
+        if c == 0:
+            @pl.when(is_gowner)
+            def _():
+                wait_bytes(grecv.at[pl.ds(0, 31)], grs_r.at[0])
+                acc = grecv[0].astype(F32)
+                for i in range(1, 32):
+                    acc = acc + grecv[i].astype(F32)
+                gall[pl.ds(pl.multiple_of(256 * t + GROWS * o, GROWS), GROWS), :] = acc.astype(BF16)
+
+                @pl.loop(0, 32)
+                def _(i):
+                    @pl.when(i != s)
+                    def _():
+                        mine = gall.at[pl.ds(pl.multiple_of(256 * t + GROWS * o, GROWS), GROWS)]
+                        copy_to(mine, mine, gag_s.at[i], gag_r.at[0], i).start()
+
         pos, right, left_id = ring_ids(c)
         far, nxt, prv = (pos + 2) % 4, (pos + 1) % 4, (pos + 3) % 4
         k = 6 * c
@@ -208,21 +242,6 @@
             ring(k + 2, part.at[c, nxt, :, bottom], rb1.at[c, 2], right),
             ring(k + 3, part.at[c, prv, :, top], rb1.at[c, 3], left_id),
         ])
-
-    @pl.when(is_gowner)
-    def _():
-        wait_bytes(grecv.at[pl.ds(0, 31)], grs_r.at[0])
-        acc = grecv[0].astype(F32)
-        for i in range(1, 32):
-            acc = acc + grecv[i].astype(F32)
-        gall[pl.ds(pl.multiple_of(256 * t + GROWS * o, GROWS), GROWS), :] = acc.astype(BF16)
-
-        @pl.loop(0, 32)
-        def _(i):
-            @pl.when(i != s)
-            def _():
-                mine = gall.at[pl.ds(pl.multiple_of(256 * t + GROWS * o, GROWS), GROWS)]
-                copy_to(mine, mine, gag_s.at[i], gag_r.at[0], i).start()
 
     def add2(a, b):
         return a.astype(F32) + b.astype(F32)
@@ -251,12 +270,19 @@
     def _():
         wait_bytes(gall.at[pl.ds(0, 256)], gag_r.at[0])
 
-    gx = []
-    for d in range(1, 4):
-        mine = gall.at[pl.ds(pl.multiple_of(256 * t, 256), 256)]
-        g = copy_to(mine, mine, gx_s.at[d], gx_r.at[d], s, (t + d) % 4)
+    def quarter(i):
+        return gall.at[pl.ds(pl.multiple_of(256 * i, 256), 256)]
+
+    lane_t = t % 2
+    sibling = t + 1 - 2 * lane_t
+    hop = (2 * h + t // 2 + 1 + 2 * lane_t) % 4
+    gx = [
+        copy_to(quarter(t), quarter(t), gx_s.at[0], gx_r.at[0],
+                z * 8 + x * 2 + hop // 2, 2 * (hop % 2) + lane_t),
+        copy_to(quarter(t), quarter(t), gx_s.at[1], gx_r.at[1], s, sibling),
+    ]
+    for g in gx:
         g.start()
-        gx.append(g)
 
     phase2 = []
     for c in range(2):
@@ -275,6 +301,9 @@
             ring(k + 2, r1.at[c, nxt, bottom], rb2.at[c, 2], right),
             ring(k + 3, r1.at[c, prv, top], rb2.at[c, 3], left_id),
         ])
+    gx[0].wait_recv()
+    gx.append(copy_to(quarter(across), quarter(across), gx_s.at[2], gx_r.at[2], s, sibling))
+    gx[2].start()
     for c in range(2):
         pos, right, left_id = ring_ids(1 - c)
         nxt, prv = (pos + 1) % 4, (pos + 3) % 4
@@ -349,8 +378,8 @@
             p = piece(k, (pa + order[n]) % 4, (pb + 3) % 4, k)
             lines[k]["a"].append(ring(base + 12 + n, p, p, rb))
 
-    for g in gx:
-        g.wait_recv()
+    gx[1].wait_recv()
+    gx[2].wait_recv()
     eye = lax.broadcasted_iota(jnp.int32, (128, 128), 0) == lax.broadcasted_iota(jnp.int32, (128, 128), 1)
 
     def unpack(src, dst, tiles, band, double):
@@ -479,7 +508,8 @@
     acc = al2[0]
     for i in range(1, 32):
         acc = acc + al2[i]
-    align_out[...] = jnp.broadcast_to(total(acc), (8, 128))
+    ratio = jnp.minimum(1.0, CLIP_LEVEL / jnp.sqrt(total(acc) / (DOUT * FF)))
+    upd_out[...] = upd_out[...] * ratio
 
     for cp in pending + gx + sums + [wp_copy, u_copy]:
         cp.wait_send()
@@ -517,20 +547,20 @@
     vmem = pltpu.VMEM
     return pl.pallas_call(
         kernel,
-        out_shape=(
-            jax.ShapeDtypeStruct((MINE, 2 * ABLK), F32),
-            jax.ShapeDtypeStruct((8, 128), F32),
-        ),
-        in_specs=[pl.BlockSpec(memory_space=pltpu.VMEM)] * 4,
-        out_specs=(pl.BlockSpec(memory_space=pltpu.VMEM),) * 2,
+        out_shape=jax.ShapeDtypeStruct((MINE, 2 * ABLK), F32),
+        in_specs=[pl.BlockSpec(memory_space=pltpu.VMEM)] + [pl.BlockSpec(memory_space=pl.ANY)] * 3,
+        out_specs=pl.BlockSpec(memory_space=pltpu.VMEM),
         scratch_shapes=[
-            vmem((2, 256, WIDTH + 640), BF16),
+            vmem((2, 256, DOUT), BF16),
+            vmem((MINE, 2 * ABLK), BF16),
+            vmem((2, 2 * ABLK, 256), BF16),
+            vmem((2, WIDTH + 640, 256), BF16),
             vmem((256, DOUT + 512), BF16),
             vmem((2, 4, 4, ROWS, BAND), BF16),
             vmem((2, NT, 32, 128), BF16),
             vmem((NT, 64, 128), BF16),
             vmem((DOUT, 128), BF16),
-            vmem((256, 128), F32),
+            vmem((128, 256), F32),
             vmem((256, GBAND), BF16),
             vmem((32, GROWS, GBAND), BF16),
             vmem((DOUT, GBAND), BF16),
@@ -560,7 +590,7 @@
             dma((57,)), dma((57,)),
             dma((4,)), dma((4,)),
             dma((32,)), dma((1,)),
-            dma((2,)), dma((2,)),
+            dma((2,)), dma((2,)), dma((3,)),
         ],
         compiler_params=pltpu.CompilerParams(
             collective_id=0, has_side_effects=True, vmem_limit_bytes=60 * 1024 * 1024),
@@ -568,9 +598,8 @@
 
 
 def per_device(hidden_acts, out_grads, sample_idx, grad_weight, momentum, weight):
-    update, alignment = whole_step(sample_idx, out_grads, grad_weight, hidden_acts)
-    ratio = jnp.minimum(1.0, CLIP_LEVEL / jnp.sqrt(alignment[0, 0] / (DOUT * FF)))
-    new_momentum = MOMENTUM_RATE * momentum + ratio * update
+    scaled = whole_step(sample_idx, out_grads, grad_weight, jnp.swapaxes(hidden_acts, 1, 2))
+    new_momentum = MOMENTUM_RATE * momentum + scaled
     new_weight = weight - LEARN_RATE * new_momentum
     return (new_momentum, new_weight)
 

time: 106 us -> 97.8 us (0.923)
  local copies, waits for them, and re-layouts: 5.73 us -> 0.01 us
  Pallas kernels: 97.1 us -> 95.1 us
    unnamed x5 -> x4, local copies, waits for them, and re-layouts: 4.54 us -> 0.01 us
    pallas_call x1, Pallas kernels: 97.1 us -> 95.1 us  [whole_step(): pl.pallas_call(kernel, out_shape=jax.ShapeDtypeStruct((MINE, 2 * ABLK), F...]
    slice x1 -> x0, local copies, waits for them, and re-layouts: 1.19 us -> none  [per_device(): alignment[0, 0] / (DOUT * FF)]
where the time goes in v2:
time: 97.8 us; the launch traced here: 97.7 us
  Pallas kernels  95.1 us (97%)
  other arithmetic  1.9 us (2%)
    pallas_call x1, Pallas kernels, whole_step(): pl.pallas_call(kernel, out_shape=jax.ShapeDtypeStruct((MINE, 2 * ABLK), F...  95.1 us

profile of v2, /device:TPU:1, one launch (start us, length us, event | category | flops | bytes accessed | tf_op | source)
XLA Modules:
  0.0 97.7 jit_solution(1888978646182034828)
XLA Ops:
  0.6 0.0 copy-start
  0.6 0.0 copy-start.1
  0.7 95.1 %shard_map.77 = f32[32,2736]{1,0:T(8,128)} custom-call(s32[2,128]{1,0:T(2,128)} %idx_ref.1, bf16[2,256,1024]{2,1,0:T(8,128)(2,1)} %grads_hbm.1, bf16[32,2736]{1,0:T(8,128)(2,1)} %w_hbm.1, bf16[2,2736,256]{2,1,0:T(8,128)(2,1)} %bitcast.1), custom_call_target="tpu_custom_call" | custom-call | tf_op jit(solution)/shard_map/pallas_call | solution.py:548
  95.7 0.0 copy-done
  95.7 0.0 copy-done.1
  95.8 1.9 %multiply_subtract_fusion = (f32[32,2736]{1,0:T(8,128)}, f32[32,2736]{1,0:T(8,128)}) fusion(f32[32,2736]{1,0:T(8,128)S(1)} %copy-done, f32[32,2736]{1,0:T(8,128)} %shard_map.77, f32[32,2736]{1,0:T(8,128)S(1)} %copy-done.1), kind=kLoop, calls=%fused_computation | loop fusion | flops 350208 | bytes 1751040 | tf_op jit(solution)/shard_map/sub | solution.py:603
Async XLA Ops:
  0.6 95.1 %copy-start = (f32[32,2736]{1,0:T(8,128)S(1)}, f32[32,2736]{1,0:T(8,128)}, u32[]{:S(2)}) copy-start(f32[32,2736]{1,0:T(8,128)} %param.11) | copy-start | bytes 1050628
  0.6 95.1 %copy-start.1 = (f32[32,2736]{1,0:T(8,128)S(1)}, f32[32,2736]{1,0:T(8,128)}, u32[]{:S(2)}) copy-start(f32[32,2736]{1,0:T(8,128)} %param.10) | copy-start | bytes 1050628

commit v3 on v2

--- a/solution.py
+++ b/solution.py
@@ -58,7 +58,7 @@
     picked, gpicked, part, w2, wpair, wc, edge,
     gq, grecv, gall, gfull,
     rb1, st1, r1, rb2, st2, r2, r3,
-    ag, sfull, vt, vfull, left, upd, ux, al, al1, al2,
+    ag, sfull, vt, vfull, left, upd, ub, ux, al, al1, al2,
     grs_s, grs_r, gag_s, gag_r, gx_s, gx_r, wa_s, wa_r, lf_s, lf_r,
     ring_s, ring_r, a1_s, a1_r, a2_s, a2_r, one_s, one_r, in_s,
 ):
@@ -96,8 +96,21 @@
 
     for d in range(1, 4):
         pl.semaphore_signal(barrier, inc=1, device_id=(s, (t + d) % 4), device_id_type=MESH)
-    across = 2 * (1 - t // 2) + t % 2
-    pl.semaphore_signal(barrier, inc=1, device_id=(pair, across), device_id_type=MESH)
+        pl.semaphore_signal(barrier, inc=1, device_id=(pair, (t + d) % 4), device_id_type=MESH)
+
+    is_gowner = h == t % 2
+    sibling = t + 1 - 2 * (t % 2)
+    along = 2 * h + t // 2
+
+    def chip(step):
+        there = (along + step) % 4
+        return z * 8 + x * 2 + there // 2, 2 * (there % 2) + there // 2
+
+    @pl.when(is_gowner)
+    def _():
+        pl.semaphore_signal(barrier, inc=1, device_id=chip(1), device_id_type=MESH)
+        pl.semaphore_signal(barrier, inc=1, device_id=chip(3), device_id_type=MESH)
+
 
     hots = []
     for m in range(2):
@@ -125,10 +138,16 @@
     w2[1, NT - 1] = edge[0:32, 0:128].astype(BF16)
     wpair[:, pl.ds(pl.multiple_of(32 * h, 32), 32), :] = w2[h]
 
-    pl.semaphore_wait(barrier, 35)
+    @pl.when(is_gowner)
+    def _():
+        pl.semaphore_wait(barrier, 39)
+
+    @pl.when(jnp.logical_not(is_gowner))
+    def _():
+        pl.semaphore_wait(barrier, 37)
+
 
     g_lane = t % 2
-    is_gowner = h == g_lane
 
     @pl.loop(0, 16)
     def _(i):
@@ -225,12 +244,12 @@
                     acc = acc + grecv[i].astype(F32)
                 gall[pl.ds(pl.multiple_of(256 * t + GROWS * o, GROWS), GROWS), :] = acc.astype(BF16)
 
-                @pl.loop(0, 32)
+                @pl.loop(0, 16)
                 def _(i):
-                    @pl.when(i != s)
+                    @pl.when(i != o)
                     def _():
                         mine = gall.at[pl.ds(pl.multiple_of(256 * t + GROWS * o, GROWS), GROWS)]
-                        copy_to(mine, mine, gag_s.at[i], gag_r.at[0], i).start()
+                        copy_to(mine, mine, gag_s.at[i], gag_r.at[0], 2 * i + h).start()
 
         pos, right, left_id = ring_ids(c)
         far, nxt, prv = (pos + 2) % 4, (pos + 1) % 4, (pos + 3) % 4
@@ -248,6 +267,22 @@
 
     def add3(a, b, c):
         return a.astype(F32) + b.astype(F32) + c.astype(F32)
+
+    def quarter(step):
+        return gall.at[pl.ds(pl.multiple_of(256 * chip(step)[1], 256), 256)]
+
+    def half_quarter(step, side):
+        return gall.at[pl.ds(pl.multiple_of(256 * chip(step)[1] + 128 * side, 128), 128)]
+
+    def along_y(k, ref, to):
+        copy_to(ref, ref, gx_s.at[k], gx_r.at[k], *to).start()
+
+    @pl.when(is_gowner)
+    def _():
+        wait_bytes(gall.at[pl.ds(0, 240)], gag_r.at[0])
+        along_y(0, quarter(0), chip(1))
+        along_y(1, quarter(0), chip(3))
+        along_y(2, quarter(0), (s, sibling))
 
     for c in range(2):
         pos, right, left_id = ring_ids(c)
@@ -261,28 +296,6 @@
         for y in range(4):
             st1[c, 1, y] = add2(rb1[c, 1, y], part[c, prv, y, HALF:ROWS]).astype(BF16)
         phase1[c].append(ring(k + 5, st1.at[c, 1], rb1.at[c, 5], left_id))
-
-    @pl.when(is_gowner)
-    def _():
-        wait_bytes(gall.at[pl.ds(0, 240)], gag_r.at[0])
-
-    @pl.when(jnp.logical_not(is_gowner))
-    def _():
-        wait_bytes(gall.at[pl.ds(0, 256)], gag_r.at[0])
-
-    def quarter(i):
-        return gall.at[pl.ds(pl.multiple_of(256 * i, 256), 256)]
-
-    lane_t = t % 2
-    sibling = t + 1 - 2 * lane_t
-    hop = (2 * h + t // 2 + 1 + 2 * lane_t) % 4
-    gx = [
-        copy_to(quarter(t), quarter(t), gx_s.at[0], gx_r.at[0],
-                z * 8 + x * 2 + hop // 2, 2 * (hop % 2) + lane_t),
-        copy_to(quarter(t), quarter(t), gx_s.at[1], gx_r.at[1], s, sibling),
-    ]
-    for g in gx:
-        g.start()
 
     phase2 = []
     for c in range(2):
@@ -301,9 +314,18 @@
             ring(k + 2, r1.at[c, nxt, bottom], rb2.at[c, 2], right),
             ring(k + 3, r1.at[c, prv, top], rb2.at[c, 3], left_id),
         ])
-    gx[0].wait_recv()
-    gx.append(copy_to(quarter(across), quarter(across), gx_s.at[2], gx_r.at[2], s, sibling))
-    gx[2].start()
+    @pl.when(is_gowner)
+    def _():
+        wait_bytes(quarter(3), gx_r.at[0])
+        along_y(3, half_quarter(3, 0), chip(1))
+        along_y(5, quarter(3), (s, sibling))
+        wait_bytes(quarter(1), gx_r.at[1])
+        along_y(4, half_quarter(1, 1), chip(3))
+        along_y(6, quarter(1), (s, sibling))
+        wait_bytes(half_quarter(2, 0), gx_r.at[3])
+        wait_bytes(half_quarter(2, 1), gx_r.at[4])
+        along_y(7, quarter(2), (s, sibling))
+
     for c in range(2):
         pos, right, left_id = ring_ids(1 - c)
         nxt, prv = (pos + 1) % 4, (pos + 3) % 4
@@ -314,6 +336,61 @@
         phase2[c][1].wait_recv()
         st2[c, 1] = add2(rb2[c, 1], r1[c, prv, HALF:ROWS]).astype(BF16)
         phase2[c].append(ring(k + 5, st2.at[c, 1], rb2.at[c, 5], left_id))
+    @pl.when(jnp.logical_not(is_gowner))
+    def _():
+        for k in (2, 5, 6, 7):
+            wait_bytes(gall.at[pl.ds(0, 256)], gx_r.at[k])
+
+    eye = lax.broadcasted_iota(jnp.int32, (128, 128), 0) == lax.broadcasted_iota(jnp.int32, (128, 128), 1)
+
+    def unpack(src, dst, tiles, band, double):
+        bands = band // 128
+        column = lax.broadcasted_iota(jnp.int32, (1, band), 1) // 128
+        weight = jnp.where(jnp.logical_and(column > 0, column <= double), 2.0, 1.0)
+
+        def body(i, carry):
+            square, trace = carry
+            at = pl.multiple_of(128 * i, 128)
+            strip = src[pl.ds(at, 128), :]
+            wide = strip.astype(F32)
+            square = square + fold_rows(wide * wide) * weight
+            trace = trace + fold_rows(jnp.where(eye, wide[:, 0:128], 0.0))
+            for k in range(bands):
+                to = pl.multiple_of(128 * ((i + k) % tiles), 128)
+                dst[pl.ds(at, 128), pl.ds(to, 128)] = strip[:, 128 * k:128 * k + 128]
+                if 1 <= k <= double:
+                    dst[pl.ds(to, 128), pl.ds(at, 128)] = wide[:, 128 * k:128 * k + 128].T.astype(BF16)
+            return square, trace
+
+        square, trace = lax.fori_loop(
+            0, tiles, body, (jnp.zeros((8, band), F32), jnp.zeros((8, 128), F32)))
+        return total(square), total(trace)
+
+    def norms(square, trace, width):
+        shift = DAMPING * trace / width
+        return shift, 1.0 / jnp.sqrt(square + 2.0 * shift * trace + shift * shift * width)
+
+    @pl.when(active)
+    def _():
+        square, trace = unpack(gall, gfull, GT, GBAND, 3)
+        shift, inv = norms(square, trace, float(DOUT))
+        wait_bytes(wc.at[pl.ds(0, 31 * 32)], wa_r.at[0])
+        y0 = wc[...].astype(F32)
+        y1 = (dot(gfull[...], wc[...]) + shift * y0) * inv
+        left[...] = y1.astype(BF16)
+        y2 = (dot(gfull[...], left[...]) + shift * y1) * inv
+        left[...] = y2.astype(BF16)
+        y3 = (dot(gfull[...], left[...]) + shift * y2) * inv
+        left[...] = (4.0 * y0 - 6.0 * y1 + 4.0 * y2 - y3).astype(BF16)
+        vt[o] = left[pl.ds(pl.multiple_of(64 * o, 64), 64), :]
+
+        @pl.loop(0, 16)
+        def _(i):
+            @pl.when(i != o)
+            def _():
+                copy_to(left.at[pl.ds(pl.multiple_of(64 * i, 64), 64)], vt.at[o],
+                        lf_s.at[i], lf_r.at[0], 2 * i + h).start()
+
     for c in range(2):
         pos, right, left_id = ring_ids(1 - c)
         for cp in phase2[c][2:]:
@@ -378,58 +455,6 @@
             p = piece(k, (pa + order[n]) % 4, (pb + 3) % 4, k)
             lines[k]["a"].append(ring(base + 12 + n, p, p, rb))
 
-    gx[1].wait_recv()
-    gx[2].wait_recv()
-    eye = lax.broadcasted_iota(jnp.int32, (128, 128), 0) == lax.broadcasted_iota(jnp.int32, (128, 128), 1)
-
-    def unpack(src, dst, tiles, band, double):
-        bands = band // 128
-        column = lax.broadcasted_iota(jnp.int32, (1, band), 1) // 128
-        weight = jnp.where(jnp.logical_and(column > 0, column <= double), 2.0, 1.0)
-
-        def body(i, carry):
-            square, trace = carry
-            at = pl.multiple_of(128 * i, 128)
-            strip = src[pl.ds(at, 128), :]
-            wide = strip.astype(F32)
-            square = square + fold_rows(wide * wide) * weight
-            trace = trace + fold_rows(jnp.where(eye, wide[:, 0:128], 0.0))
-            for k in range(bands):
-                to = pl.multiple_of(128 * ((i + k) % tiles), 128)
-                dst[pl.ds(at, 128), pl.ds(to, 128)] = strip[:, 128 * k:128 * k + 128]
-                if 1 <= k <= double:
-                    dst[pl.ds(to, 128), pl.ds(at, 128)] = wide[:, 128 * k:128 * k + 128].T.astype(BF16)
-            return square, trace
-
-        square, trace = lax.fori_loop(
-            0, tiles, body, (jnp.zeros((8, band), F32), jnp.zeros((8, 128), F32)))
-        return total(square), total(trace)
-
-    def norms(square, trace, width):
-        shift = DAMPING * trace / width
-        return shift, 1.0 / jnp.sqrt(square + 2.0 * shift * trace + shift * shift * width)
-
-    @pl.when(active)
-    def _():
-        square, trace = unpack(gall, gfull, GT, GBAND, 3)
-        shift, inv = norms(square, trace, float(DOUT))
-        wait_bytes(wc.at[pl.ds(0, 31 * 32)], wa_r.at[0])
-        y0 = wc[...].astype(F32)
-        y1 = (dot(gfull[...], wc[...]) + shift * y0) * inv
-        left[...] = y1.astype(BF16)
-        y2 = (dot(gfull[...], left[...]) + shift * y1) * inv
-        left[...] = y2.astype(BF16)
-        y3 = (dot(gfull[...], left[...]) + shift * y2) * inv
-        left[...] = (4.0 * y0 - 6.0 * y1 + 4.0 * y2 - y3).astype(BF16)
-        vt[o] = left[pl.ds(pl.multiple_of(64 * o, 64), 64), :]
-
-        @pl.loop(0, 16)
-        def _(i):
-            @pl.when(i != o)
-            def _():
-                copy_to(left.at[pl.ds(pl.multiple_of(64 * i, 64), 64)], vt.at[o],
-                        lf_s.at[i], lf_r.at[0], 2 * i + h).start()
-
     for n in range(2, 4):
         for k in range(2):
             pa = ring_ids(k)[0]
@@ -469,34 +494,39 @@
     y3 = (dot(vfull[...], sfull[...]) + shift * y2) * inv
     upd[...] = upd[...] - y3
 
-    u_copy = copy_to(upd.at[pl.ds(pl.multiple_of(32 * (1 - h), 32), 32)], ux, one_s.at[1], one_r.at[1], pair)
-    u_copy.start()
-
     wp_copy.wait_recv()
     acc = jnp.zeros((64, 128), F32)
     for j in range(NT):
         acc = acc + upd[:, 128 * j:128 * j + 128] * wpair[j].astype(F32)
     al[0] = fold_rows(acc)
-    al1[t] = al[0]
+    here = 4 * h + t
+    al1[here] = al[0]
     sums = []
-    for d in range(1, 4):
-        g = copy_to(al.at[0], al1.at[t], a1_s.at[d], a1_r.at[d], s, (t + d) % 4)
+    for d in range(1, 8):
+        there = (here + d) % 8
+        g = copy_to(al.at[0], al1.at[here], a1_s.at[d], a1_r.at[d], 2 * o + there // 4, there % 4)
         g.start()
         sums.append(g)
     for g in sums:
         g.wait_recv()
-    al[1] = (al1[0] + al1[1]) + (al1[2] + al1[3])
-    al2[s] = al[1]
-
-    @pl.loop(0, 32)
+    acc = al1[0]
+    for i in range(1, 8):
+        acc = acc + al1[i]
+    al[1] = acc
+    al2[o] = acc
+
+    @pl.loop(0, 16)
     def _(i):
-        @pl.when(i != s)
+        @pl.when(i != o)
         def _():
-            copy_to(al.at[1], al2.at[s], a2_s.at[i], a2_r.at[0], i).start()
-
+            copy_to(al.at[1], al2.at[o], a2_s.at[i], a2_r.at[0], 2 * i + h).start()
+
+    ub[...] = upd[pl.ds(pl.multiple_of(32 * (1 - h), 32), 32), :].astype(BF16)
+    u_copy = copy_to(ub, ux, one_s.at[1], one_r.at[1], pair)
+    u_copy.start()
     u_copy.wait_recv()
     own = upd[pl.ds(pl.multiple_of(32 * h, 32), 32), :]
-    other = ux[...]
+    other = ux[...].astype(F32)
     b0 = jnp.where(h == 0, own, other)
     b1 = jnp.where(h == 0, other, own)
     upd_out[:, 0:SPLIT] = b0[:, 0:SPLIT]
@@ -504,15 +534,20 @@
     upd_out[:, WIDTH:2688] = b1[:, 0:SPLIT]
     upd_out[:, 2688:2736] = b1[:, SPLIT:SPLIT + TAIL]
 
-    wait_bytes(al2.at[pl.ds(0, 31)], a2_r.at[0])
+    wait_bytes(al2.at[pl.ds(0, 15)], a2_r.at[0])
     acc = al2[0]
-    for i in range(1, 32):
+    for i in range(1, 16):
         acc = acc + al2[i]
     ratio = jnp.minimum(1.0, CLIP_LEVEL / jnp.sqrt(total(acc) / (DOUT * FF)))
     upd_out[...] = upd_out[...] * ratio
 
-    for cp in pending + gx + sums + [wp_copy, u_copy]:
+    for cp in pending + sums + [wp_copy, u_copy]:
         cp.wait_send()
+
+    @pl.when(is_gowner)
+    def _():
+        for k in range(8):
+            wait_bytes(gall.at[pl.ds(0, 128 if k in (3, 4) else 256)], gx_s.at[k])
 
     @pl.loop(0, 16)
     def _(i):
@@ -523,6 +558,14 @@
         @pl.when(jnp.logical_and(active, i != o))
         def _():
             wait_bytes(left.at[pl.ds(0, 64)], lf_s.at[i])
+
+        @pl.when(i != o)
+        def _():
+            wait_bytes(al.at[1], a2_s.at[i])
+
+        @pl.when(jnp.logical_and(is_gowner, i != o))
+        def _():
+            wait_bytes(gall.at[pl.ds(0, GROWS)], gag_s.at[i])
 
     for b in range(2):
         @pl.loop(0, NT)
@@ -530,16 +573,6 @@
             @pl.when(2 * j + b != s)
             def _():
                 wait_bytes(w2.at[b, j], wa_s.at[b * NT + j])
-
-    @pl.loop(0, 32)
-    def _(i):
-        @pl.when(i != s)
-        def _():
-            wait_bytes(al.at[1], a2_s.at[i])
-
-        @pl.when(jnp.logical_and(is_gowner, i != s))
-        def _():
-            wait_bytes(gall.at[pl.ds(0, GROWS)], gag_s.at[i])
 
 
 def whole_step(sample_idx, out_grads, grad_weight, hidden_acts):
@@ -578,18 +611,19 @@
             vmem((64, WIDTH), BF16),
             vmem((DOUT, 128), BF16),
             vmem((64, WIDTH), F32),
-            vmem((32, WIDTH), F32),
+            vmem((32, WIDTH), BF16),
+            vmem((32, WIDTH), BF16),
             vmem((2, 8, 128), F32),
-            vmem((4, 8, 128), F32),
-            vmem((32, 8, 128), F32),
+            vmem((8, 8, 128), F32),
+            vmem((16, 8, 128), F32),
             dma((16,)), dma((1,)),
-            dma((32,)), dma((1,)),
-            dma((4,)), dma((4,)),
+            dma((16,)), dma((1,)),
+            dma((8,)), dma((8,)),
             dma((2 * NT,)), dma((1,)),
             dma((16,)), dma((1,)),
             dma((57,)), dma((57,)),
-            dma((4,)), dma((4,)),
-            dma((32,)), dma((1,)),
+            dma((8,)), dma((8,)),
+            dma((16,)), dma((1,)),
             dma((2,)), dma((2,)), dma((3,)),
         ],
         compiler_params=pltpu.CompilerParams(

time: 97.8 us -> 92.6 us (0.947)
  Pallas kernels: 95.1 us -> 89.9 us
    pallas_call x1, Pallas kernels: 95.1 us -> 89.9 us  [whole_step(): pl.pallas_call(kernel, out_shape=jax.ShapeDtypeStruct((MINE, 2 * ABLK), F...]
where the time goes in v3:
time: 92.6 us; the launch traced here: 92.5 us
  Pallas kernels  89.9 us (97%)
  other arithmetic  1.9 us (2%)
    pallas_call x1, Pallas kernels, whole_step(): pl.pallas_call(kernel, out_shape=jax.ShapeDtypeStruct((MINE, 2 * ABLK), F...  89.9 us
    sub x1, other arithmetic, per_device(): new_weight = weight - LEARN_RATE * new_momentum  1.9 us

profile of v3, /device:TPU:1, one launch (start us, length us, event | category | flops | bytes accessed | tf_op | source)
XLA Modules:
  0.0 92.5 jit_solution(4683318166830648411)
XLA Ops:
  0.6 0.0 copy-start
  0.6 0.0 copy-start.1
  0.7 89.9 %shard_map.77 = f32[32,2736]{1,0:T(8,128)} custom-call(s32[2,128]{1,0:T(2,128)} %idx_ref.1, bf16[2,256,1024]{2,1,0:T(8,128)(2,1)} %grads_hbm.1, bf16[32,2736]{1,0:T(8,128)(2,1)} %w_hbm.1, bf16[2,2736,256]{2,1,0:T(8,128)(2,1)} %bitcast.1), custom_call_target="tpu_custom_call" | custom-call | tf_op jit(solution)/shard_map/pallas_call | solution.py:581
  90.5 0.0 copy-done
  90.5 0.0 copy-done.1
  90.6 1.9 %multiply_subtract_fusion = (f32[32,2736]{1,0:T(8,128)}, f32[32,2736]{1,0:T(8,128)}) fusion(f32[32,2736]{1,0:T(8,128)S(1)} %copy-done, f32[32,2736]{1,0:T(8,128)} %shard_map.77, f32[32,2736]{1,0:T(8,128)S(1)} %copy-done.1), kind=kLoop, calls=%fused_computation | loop fusion | flops 350208 | bytes 1751040 | tf_op jit(solution)/shard_map/sub | solution.py:637
Async XLA Ops:
  0.6 89.9 %copy-start = (f32[32,2736]{1,0:T(8,128)S(1)}, f32[32,2736]{1,0:T(8,128)}, u32[]{:S(2)}) copy-start(f32[32,2736]{1,0:T(8,128)} %param.11) | copy-start | bytes 1050628
  0.6 89.9 %copy-start.1 = (f32[32,2736]{1,0:T(8,128)S(1)}, f32[32,2736]{1,0:T(8,128)}, u32[]{:S(2)}) copy-start(f32[32,2736]{1,0:T(8,128)} %param.10) | copy-start | bytes 1050628

commit v4 on v3

--- a/solution.py
+++ b/solution.py
@@ -284,48 +284,47 @@
         along_y(1, quarter(0), chip(3))
         along_y(2, quarter(0), (s, sibling))
 
+    order1 = (2, 1, 3, 0)
+    combined = []
     for c in range(2):
         pos, right, left_id = ring_ids(c)
         nxt, prv = (pos + 1) % 4, (pos + 3) % 4
         k = 6 * c
+        second = ring_ids(1 - c)[0]
         phase1[c][0].wait_recv()
-        for y in range(4):
-            st1[c, 0, y] = add2(rb1[c, 0, y], part[c, nxt, y, 0:HALF]).astype(BF16)
-        phase1[c].append(ring(k + 4, st1.at[c, 0], rb1.at[c, 4], right))
         phase1[c][1].wait_recv()
-        for y in range(4):
-            st1[c, 1, y] = add2(rb1[c, 1, y], part[c, prv, y, HALF:ROWS]).astype(BF16)
-        phase1[c].append(ring(k + 5, st1.at[c, 1], rb1.at[c, 5], left_id))
-
-    phase2 = []
-    for c in range(2):
-        pos, right, left_id = ring_ids(c)
-        for cp in phase1[c][2:]:
-            cp.wait_recv()
-        for y in range(4):
-            r1[c, y, 0:HALF] = add3(part[c, pos, y, 0:HALF], rb1[c, 4, y], rb1[c, 3, y]).astype(BF16)
-            r1[c, y, HALF:ROWS] = add3(part[c, pos, y, HALF:ROWS], rb1[c, 5, y], rb1[c, 2, y]).astype(BF16)
-        pos, right, left_id = ring_ids(1 - c)
-        far, nxt, prv = (pos + 2) % 4, (pos + 1) % 4, (pos + 3) % 4
-        k = 12 + 6 * c
-        phase2.append([
-            ring(k + 0, r1.at[c, far, top], rb2.at[c, 0], right),
-            ring(k + 1, r1.at[c, far, bottom], rb2.at[c, 1], left_id),
-            ring(k + 2, r1.at[c, nxt, bottom], rb2.at[c, 2], right),
-            ring(k + 3, r1.at[c, prv, top], rb2.at[c, 3], left_id),
-        ])
-    @pl.when(is_gowner)
-    def _():
-        wait_bytes(quarter(3), gx_r.at[0])
-        along_y(3, half_quarter(3, 0), chip(1))
-        along_y(5, quarter(3), (s, sibling))
-        wait_bytes(quarter(1), gx_r.at[1])
-        along_y(4, half_quarter(1, 1), chip(3))
-        along_y(6, quarter(1), (s, sibling))
-        wait_bytes(half_quarter(2, 0), gx_r.at[3])
-        wait_bytes(half_quarter(2, 1), gx_r.at[4])
-        along_y(7, quarter(2), (s, sibling))
-
+        tail = []
+        for n, step in enumerate(order1):
+            q = (second + step) % 4
+            st1[c, 0, q] = add2(rb1[c, 0, q], part[c, nxt, q, 0:HALF]).astype(BF16)
+            st1[c, 1, q] = add2(rb1[c, 1, q], part[c, prv, q, HALF:ROWS]).astype(BF16)
+            tail.append((
+                ring(57 + 8 * c + n, st1.at[c, 0, q], rb1.at[c, 4, q], right),
+                ring(61 + 8 * c + n, st1.at[c, 1, q], rb1.at[c, 5, q], left_id),
+            ))
+        combined.append(tail)
+
+    phase2 = [[], []]
+    for n, step in enumerate(order1):
+        for c in range(2):
+            pos = ring_ids(c)[0]
+            second, right, left_id = ring_ids(1 - c)
+            q = (second + step) % 4
+            if n == 0:
+                phase1[c][2].wait_recv()
+                phase1[c][3].wait_recv()
+            combined[c][n][0].wait_recv()
+            combined[c][n][1].wait_recv()
+            r1[c, q, 0:HALF] = add3(part[c, pos, q, 0:HALF], rb1[c, 4, q], rb1[c, 3, q]).astype(BF16)
+            r1[c, q, HALF:ROWS] = add3(part[c, pos, q, HALF:ROWS], rb1[c, 5, q], rb1[c, 2, q]).astype(BF16)
+            k = 12 + 6 * c
+            if step == 2:
+                phase2[c].append(ring(k + 0, r1.at[c, q, top], rb2.at[c, 0], right))
+                phase2[c].append(ring(k + 1, r1.at[c, q, bottom], rb2.at[c, 1], left_id))
+            elif step == 1:
+                phase2[c].append(ring(k + 2, r1.at[c, q, bottom], rb2.at[c, 2], right))
+            elif step == 3:
+                phase2[c].append(ring(k + 3, r1.at[c, q, top], rb2.at[c, 3], left_id))
     for c in range(2):
         pos, right, left_id = ring_ids(1 - c)
         nxt, prv = (pos + 1) % 4, (pos + 3) % 4
@@ -336,6 +335,26 @@
         phase2[c][1].wait_recv()
         st2[c, 1] = add2(rb2[c, 1], r1[c, prv, HALF:ROWS]).astype(BF16)
         phase2[c].append(ring(k + 5, st2.at[c, 1], rb2.at[c, 5], left_id))
+    @pl.when(is_gowner)
+    def _():
+        wait_bytes(quarter(3), gx_r.at[0])
+        along_y(3, half_quarter(3, 0), chip(1))
+        along_y(5, quarter(3), (s, sibling))
+        wait_bytes(quarter(1), gx_r.at[1])
+        along_y(4, half_quarter(1, 1), chip(3))
+        along_y(6, quarter(1), (s, sibling))
+        wait_bytes(half_quarter(2, 0), gx_r.at[3])
+        wait_bytes(half_quarter(2, 1), gx_r.at[4])
+        along_y(7, quarter(2), (s, sibling))
+
+    for c in range(2):
+        pos, right, left_id = ring_ids(1 - c)
+        for cp in phase2[c][2:]:
+            cp.wait_recv()
+        r2[c, 0:HALF] = add3(r1[c, pos, 0:HALF], rb2[c, 4], rb2[c, 3]).astype(BF16)
+        r2[c, HALF:ROWS] = add3(r1[c, pos, HALF:ROWS], rb2[c, 5], rb2[c, 2]).astype(BF16)
+
+    hx = ring(24, r2.at[1 - h], r3, pair)
     @pl.when(jnp.logical_not(is_gowner))
     def _():
         for k in (2, 5, 6, 7):
@@ -391,14 +410,6 @@
                 copy_to(left.at[pl.ds(pl.multiple_of(64 * i, 64), 64)], vt.at[o],
                         lf_s.at[i], lf_r.at[0], 2 * i + h).start()
 
-    for c in range(2):
-        pos, right, left_id = ring_ids(1 - c)
-        for cp in phase2[c][2:]:
-            cp.wait_recv()
-        r2[c, 0:HALF] = add3(r1[c, pos, 0:HALF], rb2[c, 4], rb2[c, 3]).astype(BF16)
-        r2[c, HALF:ROWS] = add3(r1[c, pos, HALF:ROWS], rb2[c, 5], rb2[c, 2]).astype(BF16)
-
-    hx = ring(24, r2.at[1 - h], r3, pair)
     hx.wait_recv()
     ag[pl.ds(pl.multiple_of(ROWS * o, ROWS), ROWS), :] = add2(r2[h], r3[...]).astype(BF16)
 
@@ -621,7 +632,7 @@
             dma((8,)), dma((8,)),
             dma((2 * NT,)), dma((1,)),
             dma((16,)), dma((1,)),
-            dma((57,)), dma((57,)),
+            dma((73,)), dma((73,)),
             dma((8,)), dma((8,)),
             dma((16,)), dma((1,)),
             dma((2,)), dma((2,)), dma((3,)),

time: 92.6 us -> 91.8 us (level)
  no operation moved by 1% of the time
where the time goes in v4:
time: 91.8 us; the launch traced here: 91.6 us
  Pallas kernels  89.1 us (97%)
  other arithmetic  1.9 us (2%)
    pallas_call x1, Pallas kernels, whole_step(): pl.pallas_call(kernel, out_shape=jax.ShapeDtypeStruct((MINE, 2 * ABLK), F...  89.1 us
    sub x1, other arithmetic, per_device(): new_weight = weight - LEARN_RATE * new_momentum  1.9 us

profile of v4, /device:TPU:1, one launch (start us, length us, event | category | flops | bytes accessed | tf_op | source)
XLA Modules:
  0.0 91.6 jit_solution(4166882531628978785)
XLA Ops:
  0.6 0.0 copy-start
  0.6 0.0 copy-start.1
  0.7 89.1 %shard_map.77 = f32[32,2736]{1,0:T(8,128)} custom-call(s32[2,128]{1,0:T(2,128)} %idx_ref.1, bf16[2,256,1024]{2,1,0:T(8,128)(2,1)} %grads_hbm.1, bf16[32,2736]{1,0:T(8,128)(2,1)} %w_hbm.1, bf16[2,2736,256]{2,1,0:T(8,128)(2,1)} %bitcast.1), custom_call_target="tpu_custom_call" | custom-call | tf_op jit(solution)/shard_map/pallas_call | solution.py:592
  89.7 0.0 copy-done
  89.7 0.0 copy-done.1
  89.7 1.9 %multiply_subtract_fusion = (f32[32,2736]{1,0:T(8,128)}, f32[32,2736]{1,0:T(8,128)}) fusion(f32[32,2736]{1,0:T(8,128)S(1)} %copy-done, f32[32,2736]{1,0:T(8,128)} %shard_map.77, f32[32,2736]{1,0:T(8,128)S(1)} %copy-done.1), kind=kLoop, calls=%fused_computation | loop fusion | flops 350208 | bytes 1751040 | tf_op jit(solution)/shard_map/sub | solution.py:648
Async XLA Ops:
  0.6 89.1 %copy-start = (f32[32,2736]{1,0:T(8,128)S(1)}, f32[32,2736]{1,0:T(8,128)}, u32[]{:S(2)}) copy-start(f32[32,2736]{1,0:T(8,128)} %param.11) | copy-start | bytes 1050628
  0.6 89.1 %copy-start.1 = (f32[32,2736]{1,0:T(8,128)S(1)}, f32[32,2736]{1,0:T(8,128)}, u32[]{:S(2)}) copy-start(f32[32,2736]{1,0:T(8,128)} %param.10) | copy-start | bytes 1050628
